TPU v7x, 32 devices: a whole 2x2x4 slice. The times are simulated.
32 devices in a mesh: dp: 8 (over z, core), tensor: 4 (over y, x).
Axes of the slice: x: 2, y: 2, z: 4, core: 2. Of those that a mesh axis runs over, the one named last changes fastest.
Arguments:
- inputs: bfloat16 [8192, 2048], P(('dp', 'tensor')), may hold values from -6 to 6
- teacher: bfloat16 [8192, 2048], P(('dp', 'tensor')), may hold values from -6 to 6
- segment: int32 [8192], P('dp'), may hold values from 0 to 13, as said below
- position: int32 [8192], P('dp'), may hold values from 0 to 1023, as said below
- wq: bfloat16 [2048, 2048], P('dp', 'tensor'), may hold values from -0.125 to 0.125
- wk: bfloat16 [2048, 2048], P('dp', 'tensor'), may hold values from -0.125 to 0.125
- wv: bfloat16 [2048, 2048], P('dp', 'tensor'), may hold values from -0.125 to 0.125
- wo: bfloat16 [2048, 2048], P('tensor', 'dp'), may hold values from -0.125 to 0.125
- wg: bfloat16 [2048, 8192], P('dp', 'tensor'), may hold values from -0.125 to 0.125
- wu: bfloat16 [2048, 8192], P('dp', 'tensor'), may hold values from -0.125 to 0.125
- wd: bfloat16 [8192, 2048], P('tensor', 'dp'), may hold values from -0.0625 to 0.0625
- q_gain: bfloat16 [2048], P('dp'), may hold values from 0.099609375 to 1.8984375
- k_gain: bfloat16 [2048], P('dp'), may hold values from 0.099609375 to 1.8984375
- attn_gain: bfloat16 [2048], P('dp'), may hold values from 0.099609375 to 1.8984375
- ffn_gain: bfloat16 [2048], P('dp'), may hold values from 0.099609375 to 1.8984375
Outputs:
- output: bfloat16 [8192, 2048], P(('dp', 'tensor'))
- loss: float32 [], replicated
- grad_x: float32 [8192, 2048], P(('dp', 'tensor'))
- grad_wq: float32 [2048, 2048], P('dp', 'tensor')
- grad_wk: float32 [2048, 2048], P('dp', 'tensor')
- grad_wv: float32 [2048, 2048], P('dp', 'tensor')
- grad_wo: float32 [2048, 2048], P('tensor', 'dp')
- grad_wg: float32 [2048, 8192], P('dp', 'tensor')
- grad_wu: float32 [2048, 8192], P('dp', 'tensor')
- grad_wd: float32 [8192, 2048], P('tensor', 'dp')
- grad_q_gain: float32 [2048], P('dp')
- grad_k_gain: float32 [2048], P('dp')
- grad_attn_gain: float32 [2048], P('dp')
- grad_ffn_gain: float32 [2048], P('dp')
Inputs may be any that keep to these rules, and one draw needn't show every extreme that they name: `segment`: each sequence is 1024 consecutive tokens; in it, documents are runs of one nonzero number that never falls, followed at the sequence's end by a run of zeros (padding), which may be empty. Numbers repeat in other sequences. Sequence 0 is one whole document; sequence 1 holds thirteen. `position`: each token's index within its document; padding tokens count from the start of their padding run.
All inputs are finite; a program needn't handle non-finite values.
Results may differ from a plain program's by a relative error of at most 0.025.
Values may be sent and summed in bfloat16 or wider, within the bound.
No kernel may reach another device: no remote copies, remote signals or barrier semaphores. Data moves between devices by JAX's collectives and lax.ppermute only.
A program may use at most 192 MiB of HBM per device.

v0:
```python
import jax
import jax.numpy as jnp
from jax import lax
from jax.sharding import PartitionSpec as P

HD = 128
LEN = 1024
EPS = 1e-06
THETA = 500000.0
NEGATIVE = -1e30


def tables(position):
    freq = 1.0 / THETA ** (jnp.arange(0, HD, 2).astype(jnp.float32) / HD)
    angle = position.astype(jnp.float32)[:, None] * freq[None, :]
    angle = jnp.concatenate([angle, angle], axis=1)[:, None, :]
    return (jnp.cos(angle), jnp.sin(angle))


def rotate(values, cosines, sines):
    half = values.shape[-1] // 2
    turned = jnp.concatenate([-values[..., half:], values[..., :half]], axis=-1)
    return values * cosines + turned * sines


def unrotate(grad, cosines, sines):
    half = grad.shape[-1] // 2
    turned = grad * sines
    return grad * cosines + jnp.concatenate([turned[..., half:], -turned[..., :half]], axis=-1)


def inner_rows(left, right):
    return lax.dot_general(
        left, right, (((0,), (0,)), ((), ())), preferred_element_type=jnp.float32
    )


def times_transposed(left, right):
    return lax.dot_general(
        left, right, (((1,), (1,)), ((), ())), preferred_element_type=jnp.float32
    )


def allowed_keys(segment):
    length = segment.shape[0]
    place = lax.broadcasted_iota(jnp.int32, (length, length), 0)
    other = lax.broadcasted_iota(jnp.int32, (length, length), 1)
    return (segment[:, None] == segment[None, :]) & (place >= other)


def masked_scores(query, key, segment):
    scores = jnp.einsum(
        "qhd,khd->hqk", query, key, preferred_element_type=jnp.float32
    ) * query.shape[-1] ** (-0.5)
    return jnp.where(allowed_keys(segment)[None], scores, NEGATIVE)


def attend_forward(pack):
    query, key, value, segment = pack
    scores = masked_scores(query, key, segment)
    highest = jnp.max(scores, axis=-1, keepdims=True)
    raised = jnp.exp(scores - highest)
    total = jnp.sum(raised, axis=-1, keepdims=True)
    prob = (raised / total).astype(jnp.bfloat16)
    mixed = jnp.einsum("hqk,khd->qhd", prob, value, preferred_element_type=jnp.float32)
    return (mixed.astype(jnp.bfloat16), (highest + jnp.log(total))[..., 0])


def attend_backward(pack):
    query, key, value, segment, logsum, grad_mixed = pack
    scores = masked_scores(query, key, segment)
    prob = jnp.exp(scores - logsum[..., None])
    grad_prob = jnp.einsum("qhd,khd->hqk", grad_mixed, value, preferred_element_type=jnp.float32)
    delta = jnp.sum(grad_prob * prob, axis=-1, keepdims=True)
    grad_scores = (prob * (grad_prob - delta)).astype(jnp.bfloat16)
    factor = query.shape[-1] ** (-0.5)
    grad_value = jnp.einsum(
        "hqk,qhd->khd", prob.astype(jnp.bfloat16), grad_mixed, preferred_element_type=jnp.float32
    )
    grad_query = (
        jnp.einsum("hqk,khd->qhd", grad_scores, key, preferred_element_type=jnp.float32) * factor
    )
    grad_key = (
        jnp.einsum("hqk,qhd->khd", grad_scores, query, preferred_element_type=jnp.float32) * factor
    )
    return (grad_query, grad_key, grad_value.astype(jnp.bfloat16))


def reduce_ffn(weight_gate, weight_up, weight_down):
    return (
        lax.psum_scatter(
            weight_gate.astype(jnp.bfloat16), "dp", scatter_dimension=0, tiled=True
        ).astype(jnp.float32),
        lax.psum_scatter(
            weight_up.astype(jnp.bfloat16), "dp", scatter_dimension=0, tiled=True
        ).astype(jnp.float32),
        lax.psum_scatter(
            weight_down.astype(jnp.bfloat16), "dp", scatter_dimension=1, tiled=True
        ).astype(jnp.float32),
    )


def on_device(
    inputs,
    teacher,
    segment,
    position,
    wq,
    wk,
    wv,
    wo,
    wg,
    wu,
    wd,
    q_gain,
    k_gain,
    attn_gain,
    ffn_gain,
):
    gathered = (
        lax.all_gather(wq, "dp", axis=0, tiled=True),
        lax.all_gather(wk, "dp", axis=0, tiled=True),
        lax.all_gather(wv, "dp", axis=0, tiled=True),
        lax.all_gather(wo, "dp", axis=1, tiled=True),
        lax.all_gather(wg, "dp", axis=0, tiled=True),
        lax.all_gather(wu, "dp", axis=0, tiled=True),
        lax.all_gather(wd, "dp", axis=1, tiled=True),
        lax.all_gather(q_gain, "dp", axis=0, tiled=True),
        lax.all_gather(k_gain, "dp", axis=0, tiled=True),
        lax.all_gather(attn_gain, "dp", axis=0, tiled=True),
        lax.all_gather(ffn_gain, "dp", axis=0, tiled=True),
    )
    (
        full_q,
        full_k,
        full_v,
        full_out,
        full_gate,
        full_up,
        full_down,
        gain_q,
        gain_k,
        gain_attn,
        gain_ffn,
    ) = gathered
    rows, width = inputs.shape
    local_width = full_q.shape[1]
    heads_here = local_width // HD
    offset = lax.axis_index("tensor") * local_width
    local_gain_q = lax.dynamic_slice_in_dim(gain_q, offset, local_width).astype(jnp.float32)
    local_gain_k = lax.dynamic_slice_in_dim(gain_k, offset, local_width).astype(jnp.float32)
    norm_gain_attn = gain_attn.astype(jnp.float32)
    norm_gain_ffn = gain_ffn.astype(jnp.float32)
    cosines, sines = tables(position)
    group = segment.shape[0]
    sequences = group // LEN
    blocks = (sequences, LEN, heads_here, HD)
    segments = segment.reshape(sequences, LEN)
    whole_inputs = lax.all_gather(inputs, "tensor", axis=0, tiled=True)
    raw_q = jnp.dot(whole_inputs, full_q, preferred_element_type=jnp.float32)
    raw_k = jnp.dot(whole_inputs, full_k, preferred_element_type=jnp.float32)
    value = (
        jnp.dot(whole_inputs, full_v, preferred_element_type=jnp.float32)
        .astype(jnp.bfloat16)
        .reshape(blocks)
    )
    square_q, square_k = lax.psum(
        (jnp.sum(raw_q * raw_q, axis=1), jnp.sum(raw_k * raw_k, axis=1)), "tensor"
    )
    scale_q = lax.rsqrt(square_q / width + EPS)[:, None]
    scale_k = lax.rsqrt(square_k / width + EPS)[:, None]
    normed_q = raw_q * scale_q
    normed_k = raw_k * scale_k
    query = (
        rotate((normed_q * local_gain_q).reshape(group, heads_here, HD), cosines, sines)
        .astype(jnp.bfloat16)
        .reshape(blocks)
    )
    key = (
        rotate((normed_k * local_gain_k).reshape(group, heads_here, HD), cosines, sines)
        .astype(jnp.bfloat16)
        .reshape(blocks)
    )
    mixed, logsum = lax.map(attend_forward, (query, key, value, segments))
    attn_rows = mixed.reshape(group, local_width)
    branch_attn = lax.psum_scatter(
        jnp.dot(attn_rows, full_out, preferred_element_type=jnp.float32).astype(jnp.bfloat16),
        "tensor",
        scatter_dimension=0,
        tiled=True,
    ).astype(jnp.float32)
    scale_attn = lax.rsqrt(jnp.mean(branch_attn * branch_attn, axis=1, keepdims=True) + EPS)
    normed_attn = branch_attn * scale_attn
    resid = inputs.astype(jnp.float32) + normed_attn * norm_gain_attn
    whole_h = lax.all_gather(resid.astype(jnp.bfloat16), "tensor", axis=0, tiled=True)
    gate = jnp.dot(whole_h, full_gate, preferred_element_type=jnp.float32)
    up = jnp.dot(whole_h, full_up, preferred_element_type=jnp.float32)
    sigma = jax.nn.sigmoid(gate)
    activated = gate * sigma
    hidden = (activated * up).astype(jnp.bfloat16)
    branch_ffn = lax.psum_scatter(
        jnp.dot(hidden, full_down, preferred_element_type=jnp.float32).astype(jnp.bfloat16),
        "tensor",
        scatter_dimension=0,
        tiled=True,
    ).astype(jnp.float32)
    scale_ffn = lax.rsqrt(jnp.mean(branch_ffn * branch_ffn, axis=1, keepdims=True) + EPS)
    normed_ffn = branch_ffn * scale_ffn
    output = resid + normed_ffn * norm_gain_ffn
    my_segment = lax.dynamic_slice_in_dim(segment, lax.axis_index("tensor") * rows, rows)
    valid = (my_segment != 0).astype(jnp.float32)[:, None]
    error = output - teacher.astype(jnp.float32)
    loss_total, valid_total = lax.psum(
        (jnp.sum(valid * error * error), jnp.sum(valid)), ("dp", "tensor")
    )
    loss = loss_total / (valid_total * width)
    tokens_all = rows * lax.axis_size("dp") * lax.axis_size("tensor")
    grad_output = 2.0 * tokens_all * valid * error / valid_total
    grad_gain_ffn = jnp.sum(grad_output * normed_ffn, axis=0)
    grad_normed = grad_output * norm_gain_ffn
    grad_branch_ffn = (
        scale_ffn
        * (grad_normed - normed_ffn * jnp.mean(grad_normed * normed_ffn, axis=1, keepdims=True))
    ).astype(jnp.bfloat16)
    piece = lax.all_gather(grad_branch_ffn, "tensor", axis=0, tiled=True)
    grad_down = inner_rows(hidden, piece)
    grad_hidden = times_transposed(piece, full_down)
    grad_down, grad_hidden = (grad_down, grad_hidden)
    grad_gate = (grad_hidden * up * sigma * (1.0 + gate * (1.0 - sigma))).astype(jnp.bfloat16)
    grad_up = (grad_hidden * activated).astype(jnp.bfloat16)
    weight_gate = inner_rows(whole_h, grad_gate)
    weight_up = inner_rows(whole_h, grad_up)
    grad_resid = grad_output + lax.psum_scatter(
        (times_transposed(grad_gate, full_gate) + times_transposed(grad_up, full_up)).astype(
            jnp.bfloat16
        ),
        "tensor",
        scatter_dimension=0,
        tiled=True,
    ).astype(jnp.float32)
    ffn_sums = None
    grad_gain_attn = jnp.sum(grad_resid * normed_attn, axis=0)
    grad_normed = grad_resid * norm_gain_attn
    grad_branch_attn = (
        scale_attn
        * (grad_normed - normed_attn * jnp.mean(grad_normed * normed_attn, axis=1, keepdims=True))
    ).astype(jnp.bfloat16)
    piece = lax.all_gather(grad_branch_attn, "tensor", axis=0, tiled=True)
    grad_out_weight = inner_rows(attn_rows, piece)
    grad_mixed = times_transposed(piece, full_out)
    grad_out_weight, grad_mixed = (grad_out_weight, grad_mixed)
    grad_mixed = grad_mixed.astype(jnp.bfloat16).reshape(blocks)
    grad_query, grad_key, grad_value = lax.map(
        attend_backward, (query, key, value, segments, logsum, grad_mixed)
    )
    grad_normed_q = unrotate(grad_query.reshape(group, heads_here, HD), cosines, sines).reshape(
        group, local_width
    )
    grad_normed_k = unrotate(grad_key.reshape(group, heads_here, HD), cosines, sines).reshape(
        group, local_width
    )
    grad_value = grad_value.reshape(group, local_width)
    grad_hat_q = grad_normed_q * local_gain_q
    grad_hat_k = grad_normed_k * local_gain_k
    placed_q = lax.dynamic_update_slice_in_dim(
        jnp.zeros((width,), jnp.float32), jnp.sum(grad_normed_q * normed_q, axis=0), offset, 0
    )
    placed_k = lax.dynamic_update_slice_in_dim(
        jnp.zeros((width,), jnp.float32), jnp.sum(grad_normed_k * normed_k, axis=0), offset, 0
    )
    gain_rows = jnp.stack([placed_q, placed_k, grad_gain_attn, grad_gain_ffn])
    inner_q, inner_k, gain_rows = (
        lax.psum(jnp.sum(grad_hat_q * normed_q, axis=1).astype(jnp.bfloat16), "tensor").astype(
            jnp.float32
        ),
        lax.psum(jnp.sum(grad_hat_k * normed_k, axis=1).astype(jnp.bfloat16), "tensor").astype(
            jnp.float32
        ),
        lax.psum(gain_rows.astype(jnp.bfloat16), "tensor").astype(jnp.float32),
    )
    grad_raw_q = (scale_q * (grad_hat_q - normed_q * (inner_q / width)[:, None])).astype(
        jnp.bfloat16
    )
    grad_raw_k = (scale_k * (grad_hat_k - normed_k * (inner_k / width)[:, None])).astype(
        jnp.bfloat16
    )
    weight_q = inner_rows(whole_inputs, grad_raw_q)
    weight_k = inner_rows(whole_inputs, grad_raw_k)
    weight_v = inner_rows(whole_inputs, grad_value)
    grad_input = grad_resid + lax.psum_scatter(
        (
            times_transposed(grad_raw_q, full_q)
            + times_transposed(grad_raw_k, full_k)
            + times_transposed(grad_value, full_v)
        ).astype(jnp.bfloat16),
        "tensor",
        scatter_dimension=0,
        tiled=True,
    ).astype(jnp.float32)
    ffn_sums = reduce_ffn(weight_gate, weight_up, grad_down)
    attn_sums = (
        lax.psum_scatter(
            weight_q.astype(jnp.bfloat16), "dp", scatter_dimension=0, tiled=True
        ).astype(jnp.float32),
        lax.psum_scatter(
            weight_k.astype(jnp.bfloat16), "dp", scatter_dimension=0, tiled=True
        ).astype(jnp.float32),
        lax.psum_scatter(
            weight_v.astype(jnp.bfloat16), "dp", scatter_dimension=0, tiled=True
        ).astype(jnp.float32),
        lax.psum_scatter(
            grad_out_weight.astype(jnp.bfloat16), "dp", scatter_dimension=1, tiled=True
        ).astype(jnp.float32),
        lax.psum_scatter(
            gain_rows.astype(jnp.bfloat16), "dp", scatter_dimension=1, tiled=True
        ).astype(jnp.float32),
    )
    gains_done = attn_sums[4]
    return (
        output.astype(jnp.bfloat16),
        loss,
        grad_input,
        attn_sums[0],
        attn_sums[1],
        attn_sums[2],
        attn_sums[3],
        ffn_sums[0],
        ffn_sums[1],
        ffn_sums[2],
        gains_done[0],
        gains_done[1],
        gains_done[2],
        gains_done[3],
    )


def solution(mesh):
    placed = (
        P(("dp", "tensor"), None),
        P(("dp", "tensor"), None),
        P("dp"),
        P("dp"),
        P("dp", "tensor"),
        P("dp", "tensor"),
        P("dp", "tensor"),
        P("tensor", "dp"),
        P("dp", "tensor"),
        P("dp", "tensor"),
        P("tensor", "dp"),
        P("dp"),
        P("dp"),
        P("dp"),
        P("dp"),
    )
    return jax.shard_map(
        on_device,
        mesh=mesh,
        in_specs=placed,
        out_specs=(
            P(("dp", "tensor"), None),
            P(),
            P(("dp", "tensor"), None),
            P("dp", "tensor"),
            P("dp", "tensor"),
            P("dp", "tensor"),
            P("tensor", "dp"),
            P("dp", "tensor"),
            P("dp", "tensor"),
            P("tensor", "dp"),
            P("dp"),
            P("dp"),
            P("dp"),
            P("dp"),
        ),
        check_vma=False,
    )
```

profile of v0, /device:TPU:0, one launch (start us, length us, event | category | flops | bytes accessed | tf_op | source)
XLA Modules:
  0.0 1392.0 jit_solution(2718220709139810881)
XLA Ops:
  10.7 13.5 all-gather.1
  24.3 2.9 broadcast_multiply_fusion.1
  27.2 9.1 all-gather
  37.1 4.5 all-gather.22.cloned.1.call-done
  41.6 53.8 %all-gather.16.cloned.1.call-done = bf16[1024,2048]{1,0:T(8,128)(2,1)} async-done(((bf16[256,2048]{1,0:T(8,128)(2,1)}), bf16[1024,2048]{1,0:T(8,128)(2,1)}) %all-gather.16.cloned.1.call-update) | async-done | bytes 4194320 | tf_op jit(solution)/shard_map/all_gather | solution.py:159
  95.4 5.3 multiply_reduce_fusion.3
  100.7 25.5 %all-gather.20.cloned.1.call-done = bf16[2048,512]{1,0:T(8,128)(2,1)} async-done(((bf16[256,512]{1,0:T(8,128)(2,1)}), bf16[2048,512]{1,0:T(8,128)(2,1)}) %all-gather.20.cloned.1.call-update) | async-done | bytes 2097168 | tf_op jit(solution)/shard_map/all_gather | solution.py:121
  126.2 6.6 multiply_reduce_fusion.4
  132.8 10.0 all-reduce
  149.0 7.8 fusion.52
  156.7 5.2 convolution_convert_fusion.10
  162.0 8.7 fusion
  171.3 7.7 fusion.41
  179.1 8.6 all-gather.24.cloned.1.call-done
  187.7 6.0 convolution_convert_fusion.4
  194.6 11.7 all-gather.2
  206.3 39.3 %reduce-scatter.15.cloned.1.call-done = bf16[256,2048]{1,0:T(8,128)(2,1)} async-done(((bf16[1024,2048]{1,0:T(8,128)(2,1)}), bf16[256,2048]{1,0:T(8,128)(2,1)}) %reduce-scatter.15.cloned.1.call-update) | async-done | bytes 1048592 | tf_op jit(solution)/shard_map/reduce_scatter | solution.py:186
  247.1 2.6 fusion.40
  251.1 78.1 %all-gather.28.cloned.1.call-done = bf16[2048,2048]{1,0:T(8,128)(2,1)} async-done(((bf16[256,2048]{1,0:T(8,128)(2,1)}), bf16[2048,2048]{1,0:T(8,128)(2,1)}) %all-gather.28.cloned.1.call-update) | async-done | bytes 8388624 | tf_op jit(solution)/shard_map/all_gather | solution.py:125
  329.2 53.5 %all-gather.26.cloned.1.call-done = bf16[1024,2048]{1,0:T(8,128)(2,1)} async-done(((bf16[256,2048]{1,0:T(8,128)(2,1)}), bf16[1024,2048]{1,0:T(8,128)(2,1)}) %all-gather.26.cloned.1.call-update) | async-done | bytes 4194320 | tf_op jit(solution)/shard_map/all_gather | solution.py:195
  382.7 14.8 %fusion.53 = f32[1024,2048]{1,0:T(8,128)} fusion(bf16[1024,2048]{1,0:T(8,128)(2,1)} %all-gather.26.cloned.1.call-done, bf16[2048,2048]{1,0:T(8,128)(2,1)} %all-gather.28.cloned.1.call-done), kind=kOutput, calls=%fused_computation.129 | convolution fusion | flops 8589934592 | bytes 20971520 | tf_op jit(solution)/shard_map/dot_general | solution.py:196
  397.5 68.9 %all-gather.30.cloned.1.call-done = bf16[2048,2048]{1,0:T(8,128)(2,1)} async-done(((bf16[256,2048]{1,0:T(8,128)(2,1)}), bf16[2048,2048]{1,0:T(8,128)(2,1)}) %all-gather.30.cloned.1.call-update) | async-done | bytes 8388624 | tf_op jit(solution)/shard_map/all_gather | solution.py:126
  466.4 16.9 %multiply_convert_fusion.3 = (bf16[1024,2048]{1,0:T(8,128)(2,1)}, f32[1024,2048]{1,0:T(8,128)}) fusion(f32[1024,2048]{1,0:T(8,128)} %fusion.53, bf16[1024,2048]{1,0:T(8,128)(2,1)} %all-gather.26.cloned.1.call-done, bf16[2048,2048]{1,0:T(8,128)(2,1)} %all-gather.30.cloned.1.call-done), kind=kOutput, calls=%fused_computation.14 | convolution fusion | flops 8602517504 | bytes 33554432 | tf_op jit(solution)/shard_map/dot_general | solution.py:197
  483.3 65.5 %all-gather.32.cloned.1.call-done = bf16[2048,2048]{1,0:T(8,128)(2,1)} async-done(((bf16[2048,256]{1,0:T(8,128)(2,1)}), bf16[2048,2048]{1,0:T(8,128)(2,1)}) %all-gather.32.cloned.1.call-update) | async-done | bytes 8388624 | tf_op jit(solution)/shard_map/all_gather | solution.py:127
  548.8 13.8 convolution_convert_fusion.3
  563.4 39.7 %psum.52 = f32[]{:T(128)} all-reduce(f32[]{:T(128)} %get-tuple-element.150), channel_id=1, replica_groups=mesh['dp'=8,'tensor'=4] {'dp','tensor'}, use_global_device_ids=true, to_apply=%region_13.14 | all-reduce | flops 1 | bytes 8 | tf_op jit(solution)/shard_map/psum | solution.py:213
  603.1 10.7 all-gather.3
  616.0 5.8 fusion.31
  623.5 52.5 %all-gather.34.cloned.1.call-done = bf16[1024,2048]{1,0:T(8,128)(2,1)} async-done(((bf16[256,2048]{1,0:T(8,128)(2,1)}), bf16[1024,2048]{1,0:T(8,128)(2,1)}) %all-gather.34.cloned.1.call-update) | async-done | bytes 4194320 | tf_op jit(solution)/shard_map/all_gather | solution.py:225
  676.0 20.5 %multiply_convert_fusion.1 = (bf16[1024,2048]{1,0:T(8,128)(2,1)}, bf16[1024,2048]{1,0:T(8,128)(2,1)}) fusion(f32[1024,2048]{1,0:T(8,128)} %fusion.53, f32[1024,2048]{1,0:T(8,128)} %get-tuple-element.158, bf16[1024,2048]{1,0:T(8,128)(2,1)} %all-gather.34.cloned.1.call-done, bf16[2048,2048]{1,0:T(8,128)(2,1)} %all-gather.32.cloned.1.call-done), kind=kOutput, calls=%fused_computation.12 | convolution fusion | flops 8617197568 | bytes 37748736 | tf_op jit(solution)/shard_map/dot_general | solution.py:39
  696.5 12.7 fusion.54
  709.2 13.1 add_convert_fusion.1
  722.3 52.7 %reduce-scatter.19.cloned.1.call-done = bf16[256,2048]{1,0:T(8,128)(2,1)} async-done(((bf16[1024,2048]{1,0:T(8,128)(2,1)}), bf16[256,2048]{1,0:T(8,128)(2,1)}) %reduce-scatter.19.cloned.1.call-update) | async-done | bytes 1048592 | tf_op jit(solution)/shard_map/reduce_scatter | solution.py:233
  780.7 50.8 %all-gather.36.cloned.1.call-done = bf16[1024,2048]{1,0:T(8,128)(2,1)} async-done(((bf16[256,2048]{1,0:T(8,128)(2,1)}), bf16[1024,2048]{1,0:T(8,128)(2,1)}) %all-gather.36.cloned.1.call-update) | async-done | bytes 4194320 | tf_op jit(solution)/shard_map/all_gather | solution.py:248
  831.6 5.2 convolution_convert_fusion.9
  836.8 14.5 %multiply_reduce_fusion = (f32[4,1024]{1,0:T(4,128)}, f32[4,1024,1024]{1,2,0:T(8,128)}) fusion(f32[4,1024,1024]{1,2,0:T(8,128)} %get-tuple-element.156, f32[4,1024]{1,0:T(4,128)} %log_add_fusion, bf16[1024,4,128]{0,2,1:T(8,128)(2,1)S(1)} %bitcast.116, bf16[1024,4,128]{0,2,1:T(8,128)(2,1)} %bitcast.121), kind=kOutput, calls=%fused_computation.1 | convolution fusion | flops 1086320640 | bytes 35684352 | tf_op jit(solution)/shard_map/while/body/eval_jaxpr/qhd,khd->hqk/dot_general | solution.py:73
  853.6 8.0 multiply_convert_fusion
  864.9 6.4 bitcast_multiply_fusion.2
  877.8 14.3 %convolution_convert_fusion.2 = bf16[2048,2048]{1,0:T(8,128)(2,1)} fusion(bf16[1024,2048]{1,0:T(8,128)(2,1)} %all-gather.26.cloned.1.call-done, bf16[1024,2048]{1,0:T(8,128)(2,1)} %get-tuple-element.125), kind=kOutput, calls=%fused_computation.20 | convolution fusion | flops 8594128896 | bytes 16777216 | tf_op jit(solution)/shard_map/dot_general | solution.py:33
  892.2 14.0 %convolution_convert_fusion.1 = bf16[2048,2048]{1,0:T(8,128)(2,1)} fusion(bf16[1024,2048]{1,0:T(8,128)(2,1)} %all-gather.26.cloned.1.call-done, bf16[1024,2048]{1,0:T(8,128)(2,1)} %get-tuple-element.124), kind=kOutput, calls=%fused_computation.19 | convolution fusion | flops 8594128896 | bytes 16777216 | tf_op jit(solution)/shard_map/dot_general | solution.py:33
  906.3 14.6 %convolution_convert_fusion = bf16[2048,2048]{1,0:T(8,128)(2,1)} fusion(bf16[1024,2048]{1,0:T(8,128)(2,1)} %get-tuple-element.157, bf16[1024,2048]{1,0:T(8,128)(2,1)} %all-gather.34.cloned.1.call-done), kind=kOutput, calls=%fused_computation.18 | convolution fusion | flops 8594128896 | bytes 16777216 | tf_op jit(solution)/shard_map/dot_general | solution.py:33
  921.6 9.1 fusion.42
  931.7 3.7 fusion.10
  936.7 6.0 convolution_convert_fusion.5
  943.7 9.2 all-reduce.1
  953.0 2.9 multiply_convert_fusion.5
  956.5 3.7 fusion.8
  960.3 2.4 multiply_convert_fusion.4
  963.7 3.8 fusion.9
  969.1 2.4 fusion.56
  971.5 2.4 fusion.57
  973.9 6.0 add_convert_fusion
  980.6 40.1 %psum.51 = f32[]{:T(128)} all-reduce(f32[]{:T(128)} %get-tuple-element.115), channel_id=1, replica_groups=mesh['dp'=8,'tensor'=4] {'dp','tensor'}, use_global_device_ids=true, to_apply=%region_11.12 | all-reduce | flops 1 | bytes 8 | tf_op jit(solution)/shard_map/psum | solution.py:213
  1022.0 2.8 convert_element_type.242
  1024.8 64.7 %reduce-scatter.33.cloned.1.call-done = bf16[256,2048]{1,0:T(8,128)(2,1)} async-done(((bf16[2048,2048]{1,0:T(8,128)(2,1)}), bf16[256,2048]{1,0:T(8,128)(2,1)}) %reduce-scatter.33.cloned.1.call-update) | async-done | bytes 1048592 | tf_op jit(solution)/shard_map/reduce_scatter | solution.py:94
  1089.5 2.8 convert_element_type.244
  1092.3 87.1 %reduce-scatter.35.cloned.1.call-done = bf16[2048,256]{1,0:T(8,128)(2,1)} async-done(((bf16[2048,2048]{1,0:T(8,128)(2,1)}), bf16[2048,256]{1,0:T(8,128)(2,1)}) %reduce-scatter.35.cloned.1.call-update) | async-done | bytes 1048592 | tf_op jit(solution)/shard_map/reduce_scatter | solution.py:97
  1179.3 2.8 convert_element_type.246
  1182.1 34.0 %reduce-scatter.27.cloned.1.call-done = bf16[256,512]{0,1:T(8,128)(2,1)} async-done(((bf16[2048,512]{0,1:T(8,128)(2,1)}), bf16[256,512]{0,1:T(8,128)(2,1)}) %reduce-scatter.27.cloned.1.call-update) | async-done | bytes 262160 | tf_op jit(solution)/shard_map/reduce_scatter | solution.py:308
  1218.1 35.0 %reduce-scatter.29.cloned.1.call-done = bf16[512,256]{1,0:T(8,128)(2,1)} async-done(((bf16[512,2048]{1,0:T(8,128)(2,1)}), bf16[512,256]{1,0:T(8,128)(2,1)}) %reduce-scatter.29.cloned.1.call-update) | async-done | bytes 262160 | tf_op jit(solution)/shard_map/reduce_scatter | solution.py:311
  1254.8 35.2 %reduce-scatter.23.cloned.1.call-done = bf16[256,512]{0,1:T(8,128)(2,1)} async-done(((bf16[2048,512]{0,1:T(8,128)(2,1)}), bf16[256,512]{0,1:T(8,128)(2,1)}) %reduce-scatter.23.cloned.1.call-update) | async-done | bytes 262160 | tf_op jit(solution)/shard_map/reduce_scatter | solution.py:302
  1291.9 35.2 %reduce-scatter.25.cloned.1.call-done = bf16[256,512]{0,1:T(8,128)(2,1)} async-done(((bf16[2048,512]{0,1:T(8,128)(2,1)}), bf16[256,512]{0,1:T(8,128)(2,1)}) %reduce-scatter.25.cloned.1.call-update) | async-done | bytes 262160 | tf_op jit(solution)/shard_map/reduce_scatter | solution.py:305
  1328.9 52.3 %reduce-scatter.21.cloned.1.call-done = bf16[256,2048]{1,0:T(8,128)(2,1)} async-done(((bf16[1024,2048]{1,0:T(8,128)(2,1)}), bf16[256,2048]{1,0:T(8,128)(2,1)}) %reduce-scatter.21.cloned.1.call-update) | async-done | bytes 1048592 | tf_op jit(solution)/shard_map/reduce_scatter | solution.py:290
  1381.2 3.0 convert_add_fusion
  (227 shorter events, 52.4 us)
Async XLA Ops:
  7.2 3.5 copy-start.49
  7.2 17.0 %copy-start.43 = (s32[1024]{0:T(1024)S(1)}, s32[1024]{0:T(1024)}, u32[]{:S(2)}) copy-start(s32[1024]{0:T(1024)} %param.18) | copy-start | bytes 12292
  7.2 34.4 %all-gather.22.cloned.1.call-start = ((), (), s32[]{:S(2)}) async-start(), calls=%async_computation.15 | async-start | bytes 2359296 | tf_op jit(solution)/shard_map/all_gather | solution.py:122
  7.9 19.3 %copy-start.50 = (bf16[256]{0:T(256)(128)(2,1)S(1)}, bf16[256]{0:T(256)(128)(2,1)}, u32[]{:S(2)}) copy-start(bf16[256]{0:T(256)(128)(2,1)} %param.26) | copy-start | bytes 1540
  7.9 28.6 %copy-start.42 = (s32[1024]{0:T(1024)S(1)}, s32[1024]{0:T(1024)}, u32[]{:S(2)}) copy-start(s32[1024]{0:T(1024)} %param.17) | copy-start | bytes 12292
  8.0 87.5 %all-gather.16.cloned.1.call-start = ((), (), s32[]{:S(2)}) async-start(), calls=%async_computation.12 | async-start | bytes 5242880 | tf_op jit(solution)/shard_map/all_gather | solution.py:159
  8.7 117.5 %all-gather.20.cloned.1.call-start = ((), (), s32[]{:S(2)}) async-start(), calls=%async_computation.14 | async-start | bytes 2359296 | tf_op jit(solution)/shard_map/all_gather | solution.py:121
  9.4 147.3 %all-gather.18.cloned.1.call-start = ((), (), s32[]{:S(2)}) async-start(), calls=%async_computation.13 | async-start | bytes 2359296 | tf_op jit(solution)/shard_map/all_gather | solution.py:123
  10.0 177.7 %all-gather.24.cloned.1.call-start = ((), (), s32[]{:S(2)}) async-start(), calls=%async_computation.16 | async-start | bytes 2359296 | tf_op jit(solution)/shard_map/all_gather | solution.py:124
  10.6 235.0 %reduce-scatter.15.cloned.1.call-start = ((), (), s32[]{:S(2)}) async-start(), calls=%async_computation.17 | async-start | bytes 5242880 | tf_op jit(solution)/shard_map/reduce_scatter | solution.py:186
  36.4 106.3 %copy-start.35 = (f32[512]{0:T(512)}, f32[512]{0:T(512)S(1)}, u32[]{:S(2)}) copy-start(f32[512]{0:T(512)S(1)} %dynamic-slice_convert_fusion) | copy-start | bytes 6148
  36.5 107.1 %copy-start.37 = (f32[512]{0:T(512)}, f32[512]{0:T(512)S(1)}, u32[]{:S(2)}) copy-start(f32[512]{0:T(512)S(1)} %dynamic-slice_convert_fusion.1) | copy-start | bytes 6148
  100.7 42.1 %copy-start.5 = (f32[1024,512]{0,1:T(8,128)}, f32[1024,512]{0,1:T(8,128)S(1)}, u32[]{:S(2)}) copy-start(f32[1024,512]{0,1:T(8,128)S(1)} %get-tuple-element.152) | copy-start | bytes 6291460
  143.4 1.6 copy-start.7
  156.7 14.0 %copy-start.27 = (f32[4,1024]{1,0:T(4,128)}, f32[4,1024]{1,0:T(4,128)S(1)}, u32[]{:S(2)}) copy-start(f32[4,1024]{1,0:T(4,128)S(1)} %get-tuple-element.155) | copy-start | bytes 49156
  162.0 8.8 copy-start.19
  179.1 14.7 %copy-start.53 = (bf16[4,128,1024]{2,1,0:T(8,128)(2,1)}, bf16[4,128,1024]{2,1,0:T(8,128)(2,1)S(1)}, u32[]{:S(2)}) copy-start(bf16[4,128,1024]{2,1,0:T(8,128)(2,1)S(1)} %fusion.41) | copy-start | bytes 3145732
  193.8 53.3 %copy-start.13 = (bf16[256,2048]{1,0:T(8,128)(2,1)S(1)}, bf16[256,2048]{1,0:T(8,128)(2,1)}, u32[]{:S(2)}) copy-start(bf16[256,2048]{1,0:T(8,128)(2,1)} %param.15) | copy-start | bytes 3145732
  193.8 135.4 %all-gather.28.cloned.1.call-start = ((), (), s32[]{:S(2)}) async-start(), calls=%async_computation.19 | async-start | bytes 9437184 | tf_op jit(solution)/shard_map/all_gather | solution.py:125
  194.5 188.2 %all-gather.26.cloned.1.call-start = ((), (), s32[]{:S(2)}) async-start(), calls=%async_computation.18 | async-start | bytes 5242880 | tf_op jit(solution)/shard_map/all_gather | solution.py:195
  249.8 216.6 %all-gather.30.cloned.1.call-start = ((), (), s32[]{:S(2)}) async-start(), calls=%async_computation.20 | async-start | bytes 9437184 | tf_op jit(solution)/shard_map/all_gather | solution.py:126
  250.5 298.3 %all-gather.32.cloned.1.call-start = ((), (), s32[]{:S(2)}) async-start(), calls=%async_computation.21 | async-start | bytes 9437184 | tf_op jit(solution)/shard_map/all_gather | solution.py:127
  251.1 363.4 %reduce-scatter.17.cloned.1.call-start = ((), (), s32[]{:S(2)}) async-start(), calls=%async_computation.22 | async-start | bytes 5242880 | tf_op jit(solution)/shard_map/reduce_scatter | solution.py:201
  562.7 40.5 %copy-start.52 = (bf16[256]{0:T(256)(128)(2,1)S(1)}, bf16[256]{0:T(256)(128)(2,1)}, u32[]{:S(2)}) copy-start(bf16[256]{0:T(256)(128)(2,1)} %param.29) | copy-start | bytes 1540
  562.7 53.3 %copy-start.3 = (bf16[256,2048]{1,0:T(8,128)(2,1)S(1)}, bf16[256,2048]{1,0:T(8,128)(2,1)}, u32[]{:S(2)}) copy-start(bf16[256,2048]{1,0:T(8,128)(2,1)} %reduce-scatter.15.cloned.1.call-done) | copy-start | bytes 3145732
  562.7 113.3 %all-gather.34.cloned.1.call-start = ((), (), s32[]{:S(2)}) async-start(), calls=%async_computation.23 | async-start | bytes 5242880 | tf_op jit(solution)/shard_map/all_gather | solution.py:225
  616.0 5.8 copy-start.16
  621.8 155.4 %copy-start.1 = (f32[256,2048]{1,0:T(8,128)}, f32[256,2048]{1,0:T(8,128)S(1)}, u32[]{:S(2)}) copy-start(f32[256,2048]{1,0:T(8,128)S(1)} %get-tuple-element.121) | copy-start | bytes 6291460
  623.5 151.5 %reduce-scatter.19.cloned.1.call-start = ((), (), s32[]{:S(2)}) async-start(), calls=%async_computation.24 | async-start | bytes 5242880 | tf_op jit(solution)/shard_map/reduce_scatter | solution.py:233
  696.5 12.7 copy-start.55
  722.3 109.3 %all-gather.36.cloned.1.call-start = ((), (), s32[]{:S(2)}) async-start(), calls=%async_computation.25 | async-start | bytes 5242880 | tf_op jit(solution)/shard_map/all_gather | solution.py:248
  775.0 2.2 copy-start.14
  777.2 1.7 copy-start.28
  777.2 1.7 copy-start.34
  778.8 163.9 %reduce-scatter.37.cloned.1.call-start = ((), (), s32[]{:S(2)}) async-start(), calls=%async_computation.34 | async-start | bytes 589824
  836.8 14.6 %slice-start = ((s8[16777216]{0:T(1024)(128)(4,1)}), s8[4194304]{0:T(1024)(128)(4,1)S(1)}, s32[]{:S(2)}) async-start(s8[16777216]{0:T(1024)(128)(4,1)} %bitcast.110), calls=%async_computation.35 | async-start | bytes 8388608
  836.8 14.6 %slice-start.1 = ((s8[16777216]{0:T(1024)(128)(4,1)}), s8[4194304]{0:T(1024)(128)(4,1)S(1)}, s32[]{:S(2)}) async-start(s8[16777216]{0:T(1024)(128)(4,1)} %bitcast.110), calls=%async_computation.36 | async-start | bytes 8388608
  836.8 15.6 %slice-start.2 = ((s8[16777216]{0:T(1024)(128)(4,1)}), s8[4194304]{0:T(1024)(128)(4,1)S(1)}, s32[]{:S(2)}) async-start(s8[16777216]{0:T(1024)(128)(4,1)} %bitcast.110), calls=%async_computation.37 | async-start | bytes 8388608
  836.8 16.7 %slice-start.3 = ((s8[16777216]{0:T(1024)(128)(4,1)}), s8[4194304]{0:T(1024)(128)(4,1)S(1)}, s32[]{:S(2)}) async-start(s8[16777216]{0:T(1024)(128)(4,1)} %bitcast.110), calls=%async_computation.38 | async-start | bytes 8388608
  853.6 8.0 copy-start.12
  861.6 3.3 copy-start
  861.6 3.3 copy-start.10
  861.6 3.3 copy-start.21
  874.1 1.8 copy-start.6
  874.1 1.8 copy-start.30
  874.1 1.8 copy-start.36
  877.7 144.2 %reduce-scatter.31.cloned.1.call-start = ((), (), s32[]{:S(2)}) async-start(), calls=%async_computation.31 | async-start | bytes 9437184 | tf_op jit(solution)/shard_map/reduce_scatter | solution.py:91
  892.2 197.3 %reduce-scatter.33.cloned.1.call-start = ((), (), s32[]{:S(2)}) async-start(), calls=%async_computation.32 | async-start | bytes 9437184 | tf_op jit(solution)/shard_map/reduce_scatter | solution.py:94
  906.3 273.0 %reduce-scatter.35.cloned.1.call-start = ((), (), s32[]{:S(2)}) async-start(), calls=%async_computation.33 | async-start | bytes 9437184 | tf_op jit(solution)/shard_map/reduce_scatter | solution.py:97
  920.9 295.3 %reduce-scatter.27.cloned.1.call-start = ((), (), s32[]{:S(2)}) async-start(), calls=%async_computation.29 | async-start | bytes 2359296 | tf_op jit(solution)/shard_map/reduce_scatter | solution.py:308
  921.6 10.1 copy-start.44
  935.5 317.6 %reduce-scatter.29.cloned.1.call-start = ((), (), s32[]{:S(2)}) async-start(), calls=%async_computation.30 | async-start | bytes 2359296 | tf_op jit(solution)/shard_map/reduce_scatter | solution.py:311
  942.7 10.3 copy-start.39
  942.7 347.3 %reduce-scatter.23.cloned.1.call-start = ((), (), s32[]{:S(2)}) async-start(), calls=%async_computation.27 | async-start | bytes 2359296 | tf_op jit(solution)/shard_map/reduce_scatter | solution.py:302
  952.9 3.5 copy-start.45
  960.2 366.8 %reduce-scatter.25.cloned.1.call-start = ((), (), s32[]{:S(2)}) async-start(), calls=%async_computation.28 | async-start | bytes 2359296 | tf_op jit(solution)/shard_map/reduce_scatter | solution.py:305
  960.3 3.4 copy-start.46
  967.4 1.7 copy-start.48
  967.5 413.8 %reduce-scatter.21.cloned.1.call-start = ((), (), s32[]{:S(2)}) async-start(), calls=%async_computation.26 | async-start | bytes 5242880 | tf_op jit(solution)/shard_map/reduce_scatter | solution.py:290
  969.1 2.4 copy-start.25
  969.1 2.4 copy-start.47
  971.5 2.4 copy-start.18
  1179.3 201.9 %copy-start.15 = (bf16[256,2048]{1,0:T(8,128)(2,1)S(1)}, bf16[256,2048]{1,0:T(8,128)(2,1)}, u32[]{:S(2)}) copy-start(bf16[256,2048]{1,0:T(8,128)(2,1)} %reduce-scatter.19.cloned.1.call-done) | copy-start | bytes 3145732
  1182.1 199.1 %copy-start.2 = (f32[256,2048]{1,0:T(8,128)S(1)}, f32[256,2048]{1,0:T(8,128)}, u32[]{:S(2)}) copy-start(f32[256,2048]{1,0:T(8,128)} %copy-done.1) | copy-start | bytes 6291460
  (19 other events, 19.9 us)
Sparse Core Ops, SparseCore 0:
  9.6 31.9 all-gather.21
  43.4 51.9 all-gather.15
  97.0 29.1 all-gather.19
  127.7 28.5 all-gather.17
  157.7 29.9 all-gather.23
  193.9 51.6 reduce-scatter.14
  247.2 82.0 all-gather.27
  331.6 51.0 all-gather.25
  384.3 82.0 all-gather.29
  467.8 80.9 all-gather.31
  562.8 51.5 reduce-scatter.16
  623.6 52.3 all-gather.33
  722.4 52.5 reduce-scatter.18
  779.0 52.5 all-gather.35
  877.9 31.4 reduce-scatter.36
  911.5 87.6 reduce-scatter.30
  1001.4 88.0 reduce-scatter.32
  1091.6 87.6 reduce-scatter.34
  1181.6 34.5 reduce-scatter.26
  1218.3 34.6 reduce-scatter.28
  1255.3 34.5 reduce-scatter.22
  1292.3 34.6 reduce-scatter.24
  1330.0 51.1 reduce-scatter.20
where the time goes:
time: 1400 us; the launch traced here: 1390 us
  waiting for transfers between devices  903 us (64%)
  matrix products  238 us (17%)
  blocking collectives  144 us (10%)
  other arithmetic  62 us (4%)
  local copies, waits for them, and re-layouts  26.9 us (2%)
  between operations  17.5 us (1%)
    reduce_scatter x1, waiting for transfers between devices, reduce_ffn(): lax.psum_scatter(weight_down.astype(jnp.bfloat16), 'dp', scatter_dimensio...  87.1 us
    psum x2, blocking collectives, on_device(): lax.psum((jnp.sum(valid * error * error), jnp.sum(valid)), ('dp', 'tensor'))  79.8 us
    all_gather x1, waiting for transfers between devices, on_device(): lax.all_gather(wg, 'dp', axis=0, tiled=True)  78.1 us
    all_gather x1, waiting for transfers between devices, on_device(): lax.all_gather(wu, 'dp', axis=0, tiled=True)  68.9 us
    all_gather x1, waiting for transfers between devices, on_device(): lax.all_gather(wd, 'dp', axis=1, tiled=True)  65.5 us
    reduce_scatter x1, waiting for transfers between devices, reduce_ffn(): lax.psum_scatter(weight_up.astype(jnp.bfloat16), 'dp', scatter_dimension=...  64.7 us
    dot_general x7, matrix products, times_transposed(): lax.dot_general(left, right, (((1,), (1,)), ((), ())), preferred_element_...  62.3 us
    dot_general x7, matrix products, inner_rows(): lax.dot_general(left, right, (((0,), (0,)), ((), ())), preferred_element_...  60.1 us
  transfers between devices with their start and end apart: 23, of which 20 were waited for; matrix products, arithmetic and copies ran while one was open for 14% of the time, Pallas kernels for 0%

commit v1 on v0

--- a/solution.py
+++ b/solution.py
@@ -192,7 +192,10 @@
     scale_attn = lax.rsqrt(jnp.mean(branch_attn * branch_attn, axis=1, keepdims=True) + EPS)
     normed_attn = branch_attn * scale_attn
     resid = inputs.astype(jnp.float32) + normed_attn * norm_gain_attn
-    whole_h = lax.all_gather(resid.astype(jnp.bfloat16), "tensor", axis=0, tiled=True)
+    unite_works = lambda z: jnp.concatenate(
+        lax.all_to_all(jnp.stack([z for _ in range(lax.axis_size("tensor"))], 0), "tensor", 0, 0), 0
+    )
+    whole_h = unite_works(resid.astype(jnp.bfloat16))
     gate = jnp.dot(whole_h, full_gate, preferred_element_type=jnp.float32)
     up = jnp.dot(whole_h, full_up, preferred_element_type=jnp.float32)
     sigma = jax.nn.sigmoid(gate)

time: 1400 us -> 1350 us (0.964)
  waiting for transfers between devices: 903 us -> 841 us
    all_gather x1 -> x0, waiting for transfers between devices: 53.5 us -> none  [on_device(): lax.all_gather(resid.astype(jnp.bfloat16), 'tensor', axis=0, tiled=True)]
  transfers between devices with their start and end apart: 23 -> 23, of which waited for: 20 -> 19; matrix products, arithmetic and copies ran while one was open for 14% -> 14% of each run, Pallas kernels for 0% -> 0%
where the time goes in v1:
time: 1350 us; the launch traced here: 1340 us
  waiting for transfers between devices  841 us (62%)
  matrix products  238 us (18%)
  blocking collectives  144 us (11%)
  other arithmetic  61.2 us (5%)
  local copies, waits for them, and re-layouts  29.4 us (2%)
  between operations  17.8 us (1%)
    reduce_scatter x1, waiting for transfers between devices, reduce_ffn(): lax.psum_scatter(weight_down.astype(jnp.bfloat16), 'dp', scatter_dimensio...  87 us
    psum x2, blocking collectives, on_device(): lax.psum((jnp.sum(valid * error * error), jnp.sum(valid)), ('dp', 'tensor'))  79.8 us
    all_gather x1, waiting for transfers between devices, on_device(): lax.all_gather(wg, 'dp', axis=0, tiled=True)  72.8 us
    all_gather x1, waiting for transfers between devices, on_device(): lax.all_gather(wu, 'dp', axis=0, tiled=True)  67.5 us
    all_gather x1, waiting for transfers between devices, on_device(): lax.all_gather(wd, 'dp', axis=1, tiled=True)  65.6 us
    reduce_scatter x1, waiting for transfers between devices, reduce_ffn(): lax.psum_scatter(weight_up.astype(jnp.bfloat16), 'dp', scatter_dimension=...  64.7 us
    dot_general x7, matrix products, times_transposed(): lax.dot_general(left, right, (((1,), (1,)), ((), ())), preferred_element_...  62.3 us
    dot_general x7, matrix products, inner_rows(): lax.dot_general(left, right, (((0,), (0,)), ((), ())), preferred_element_...  60.1 us
  transfers between devices with their start and end apart: 23, of which 19 were waited for; matrix products, arithmetic and copies ran while one was open for 14% of the time, Pallas kernels for 0%

profile of v1, /device:TPU:0, one launch (start us, length us, event | category | flops | bytes accessed | tf_op | source)
XLA Modules:
  0.0 1337.2 jit_solution(17056650839619746163)
XLA Ops:
  10.7 13.5 %all-gather.1 = bf16[8,1,256]{2,1,0:T(2,128)(2,1)S(1)} all-gather(bf16[1,1,256]{2,1,0:T(2,128)(2,1)S(1)} %reshape.231), channel_id=1, replica_groups=mesh['dp'=8,'tensor'=4] {'dp'}, dimensions={0}, use_global_device_ids=true | all-gather | bytes 4608 | tf_op jit(solution)/shard_map/all_gather | solution.py:129
  24.3 2.9 broadcast_multiply_fusion.1
  27.2 9.1 all-gather
  37.1 4.5 all-gather.21.cloned.1.call-done
  41.6 53.8 %all-gather.15.cloned.1.call-done = bf16[1024,2048]{1,0:T(8,128)(2,1)} async-done(((bf16[256,2048]{1,0:T(8,128)(2,1)}), bf16[1024,2048]{1,0:T(8,128)(2,1)}) %all-gather.15.cloned.1.call-update) | async-done | bytes 4194320 | tf_op jit(solution)/shard_map/all_gather | solution.py:159
  95.4 5.3 multiply_reduce_fusion.3
  100.7 25.5 %all-gather.19.cloned.1.call-done = bf16[2048,512]{1,0:T(8,128)(2,1)} async-done(((bf16[256,512]{1,0:T(8,128)(2,1)}), bf16[2048,512]{1,0:T(8,128)(2,1)}) %all-gather.19.cloned.1.call-update) | async-done | bytes 2097168 | tf_op jit(solution)/shard_map/all_gather | solution.py:121
  126.2 6.6 multiply_reduce_fusion.4
  132.8 10.0 all-reduce
  149.0 7.7 fusion.52
  156.7 5.2 convolution_convert_fusion.10
  162.0 8.7 fusion
  171.3 7.7 fusion.41
  179.1 8.7 all-gather.23.cloned.1.call-done
  187.7 6.0 convolution_convert_fusion.4
  196.0 11.7 all-gather.2
  207.7 37.8 %reduce-scatter.15.cloned.1.call-done = bf16[256,2048]{1,0:T(8,128)(2,1)} async-done(((bf16[1024,2048]{1,0:T(8,128)(2,1)}), bf16[256,2048]{1,0:T(8,128)(2,1)}) %reduce-scatter.15.cloned.1.call-update) | async-done | bytes 1048592 | tf_op jit(solution)/shard_map/reduce_scatter | solution.py:186
  248.8 2.5 stack.27
  251.3 5.0 all-to-all-start
  256.4 72.8 %all-gather.25.cloned.1.call-done = bf16[2048,2048]{1,0:T(8,128)(2,1)} async-done(((bf16[256,2048]{1,0:T(8,128)(2,1)}), bf16[2048,2048]{1,0:T(8,128)(2,1)}) %all-gather.25.cloned.1.call-update) | async-done | bytes 8388624 | tf_op jit(solution)/shard_map/all_gather | solution.py:125
  329.2 14.7 %fusion.53 = f32[1024,2048]{1,0:T(8,128)} fusion(bf16[1024,2048]{1,0:T(8,128)(2,1)} %bitcast.6, bf16[2048,2048]{1,0:T(8,128)(2,1)} %all-gather.25.cloned.1.call-done), kind=kOutput, calls=%fused_computation.129 | convolution fusion | flops 8589934592 | bytes 20971520 | tf_op jit(solution)/shard_map/dot_general | solution.py:199
  343.8 67.5 %all-gather.27.cloned.1.call-done = bf16[2048,2048]{1,0:T(8,128)(2,1)} async-done(((bf16[256,2048]{1,0:T(8,128)(2,1)}), bf16[2048,2048]{1,0:T(8,128)(2,1)}) %all-gather.27.cloned.1.call-update) | async-done | bytes 8388624 | tf_op jit(solution)/shard_map/all_gather | solution.py:126
  411.3 17.0 %multiply_convert_fusion.3 = (bf16[1024,2048]{1,0:T(8,128)(2,1)}, f32[1024,2048]{1,0:T(8,128)}) fusion(f32[1024,2048]{1,0:T(8,128)} %fusion.53, bf16[1024,2048]{1,0:T(8,128)(2,1)} %bitcast.6, bf16[2048,2048]{1,0:T(8,128)(2,1)} %all-gather.27.cloned.1.call-done), kind=kOutput, calls=%fused_computation.14 | convolution fusion | flops 8602517504 | bytes 33554432 | tf_op jit(solution)/shard_map/dot_general | solution.py:200
  428.3 65.6 %all-gather.29.cloned.1.call-done = bf16[2048,2048]{1,0:T(8,128)(2,1)} async-done(((bf16[2048,256]{1,0:T(8,128)(2,1)}), bf16[2048,2048]{1,0:T(8,128)(2,1)}) %all-gather.29.cloned.1.call-update) | async-done | bytes 8388624 | tf_op jit(solution)/shard_map/all_gather | solution.py:127
  493.9 13.9 %convolution_convert_fusion.3 = bf16[1024,2048]{1,0:T(8,128)(2,1)} fusion(bf16[1024,2048]{1,0:T(8,128)(2,1)} %get-tuple-element.157, bf16[2048,2048]{1,0:T(8,128)(2,1)} %all-gather.29.cloned.1.call-done), kind=kOutput, calls=%fused_computation.23 | convolution fusion | flops 8592031744 | bytes 16777216 | tf_op jit(solution)/shard_map/dot_general | solution.py:205
  508.5 39.7 %psum.52 = f32[]{:T(128)} all-reduce(f32[]{:T(128)} %get-tuple-element.150), channel_id=1, replica_groups=mesh['dp'=8,'tensor'=4] {'dp','tensor'}, use_global_device_ids=true, to_apply=%region_13.14 | all-reduce | flops 1 | bytes 8 | tf_op jit(solution)/shard_map/psum | solution.py:216
  548.2 10.7 all-gather.3
  561.1 5.8 fusion.31
  568.6 52.5 %all-gather.31.cloned.1.call-done = bf16[1024,2048]{1,0:T(8,128)(2,1)} async-done(((bf16[256,2048]{1,0:T(8,128)(2,1)}), bf16[1024,2048]{1,0:T(8,128)(2,1)}) %all-gather.31.cloned.1.call-update) | async-done | bytes 4194320 | tf_op jit(solution)/shard_map/all_gather | solution.py:228
  621.1 20.5 %multiply_convert_fusion.1 = (bf16[1024,2048]{1,0:T(8,128)(2,1)}, bf16[1024,2048]{1,0:T(8,128)(2,1)}) fusion(f32[1024,2048]{1,0:T(8,128)} %fusion.53, f32[1024,2048]{1,0:T(8,128)} %get-tuple-element.158, bf16[1024,2048]{1,0:T(8,128)(2,1)} %all-gather.31.cloned.1.call-done, bf16[2048,2048]{1,0:T(8,128)(2,1)} %all-gather.29.cloned.1.call-done), kind=kOutput, calls=%fused_computation.12 | convolution fusion | flops 8617197568 | bytes 37748736 | tf_op jit(solution)/shard_map/dot_general | solution.py:39
  641.6 12.7 fusion.54
  654.3 13.1 add_convert_fusion.1
  667.5 52.7 %reduce-scatter.19.cloned.1.call-done = bf16[256,2048]{1,0:T(8,128)(2,1)} async-done(((bf16[1024,2048]{1,0:T(8,128)(2,1)}), bf16[256,2048]{1,0:T(8,128)(2,1)}) %reduce-scatter.19.cloned.1.call-update) | async-done | bytes 1048592 | tf_op jit(solution)/shard_map/reduce_scatter | solution.py:236
  725.9 50.8 %all-gather.33.cloned.1.call-done = bf16[1024,2048]{1,0:T(8,128)(2,1)} async-done(((bf16[256,2048]{1,0:T(8,128)(2,1)}), bf16[1024,2048]{1,0:T(8,128)(2,1)}) %all-gather.33.cloned.1.call-update) | async-done | bytes 4194320 | tf_op jit(solution)/shard_map/all_gather | solution.py:251
  776.7 5.2 convolution_convert_fusion.9
  782.0 14.5 %multiply_reduce_fusion = (f32[4,1024]{1,0:T(4,128)}, f32[4,1024,1024]{1,2,0:T(8,128)}) fusion(f32[4,1024,1024]{1,2,0:T(8,128)} %get-tuple-element.156, f32[4,1024]{1,0:T(4,128)} %log_add_fusion, bf16[1024,4,128]{0,2,1:T(8,128)(2,1)S(1)} %bitcast.117, bf16[1024,4,128]{0,2,1:T(8,128)(2,1)} %bitcast.122), kind=kOutput, calls=%fused_computation.1 | convolution fusion | flops 1086320640 | bytes 35684352 | tf_op jit(solution)/shard_map/while/body/eval_jaxpr/qhd,khd->hqk/dot_general | solution.py:73
  798.8 8.0 multiply_convert_fusion
  810.1 6.4 bitcast_multiply_fusion.2
  823.0 14.4 %convolution_convert_fusion.2 = bf16[2048,2048]{1,0:T(8,128)(2,1)} fusion(bf16[1024,2048]{1,0:T(8,128)(2,1)} %bitcast.6, bf16[1024,2048]{1,0:T(8,128)(2,1)} %get-tuple-element.125), kind=kOutput, calls=%fused_computation.20 | convolution fusion | flops 8594128896 | bytes 16777216 | tf_op jit(solution)/shard_map/dot_general | solution.py:33
  837.4 14.1 %convolution_convert_fusion.1 = bf16[2048,2048]{1,0:T(8,128)(2,1)} fusion(bf16[1024,2048]{1,0:T(8,128)(2,1)} %bitcast.6, bf16[1024,2048]{1,0:T(8,128)(2,1)} %get-tuple-element.124), kind=kOutput, calls=%fused_computation.19 | convolution fusion | flops 8594128896 | bytes 16777216 | tf_op jit(solution)/shard_map/dot_general | solution.py:33
  851.5 14.5 %convolution_convert_fusion = bf16[2048,2048]{1,0:T(8,128)(2,1)} fusion(bf16[1024,2048]{1,0:T(8,128)(2,1)} %get-tuple-element.157, bf16[1024,2048]{1,0:T(8,128)(2,1)} %all-gather.31.cloned.1.call-done), kind=kOutput, calls=%fused_computation.18 | convolution fusion | flops 8594128896 | bytes 16777216 | tf_op jit(solution)/shard_map/dot_general | solution.py:33
  866.8 9.1 fusion.42
  876.9 3.7 fusion.10
  881.9 6.0 convolution_convert_fusion.5
  888.9 9.2 all-reduce.1
  898.1 2.9 multiply_convert_fusion.5
  901.7 3.7 fusion.8
  905.4 2.4 multiply_convert_fusion.4
  908.8 3.8 fusion.9
  914.3 2.4 fusion.56
  916.7 2.4 fusion.57
  919.1 6.0 add_convert_fusion
  925.8 40.1 %psum.51 = f32[]{:T(128)} all-reduce(f32[]{:T(128)} %get-tuple-element.115), channel_id=1, replica_groups=mesh['dp'=8,'tensor'=4] {'dp','tensor'}, use_global_device_ids=true, to_apply=%region_11.12 | all-reduce | flops 1 | bytes 8 | tf_op jit(solution)/shard_map/psum | solution.py:216
  967.1 2.8 convert_element_type.242
  969.9 64.7 %reduce-scatter.33.cloned.1.call-done = bf16[256,2048]{1,0:T(8,128)(2,1)} async-done(((bf16[2048,2048]{1,0:T(8,128)(2,1)}), bf16[256,2048]{1,0:T(8,128)(2,1)}) %reduce-scatter.33.cloned.1.call-update) | async-done | bytes 1048592 | tf_op jit(solution)/shard_map/reduce_scatter | solution.py:94
  1034.7 2.8 convert_element_type.244
  1037.4 87.0 %reduce-scatter.35.cloned.1.call-done = bf16[2048,256]{1,0:T(8,128)(2,1)} async-done(((bf16[2048,2048]{1,0:T(8,128)(2,1)}), bf16[2048,256]{1,0:T(8,128)(2,1)}) %reduce-scatter.35.cloned.1.call-update) | async-done | bytes 1048592 | tf_op jit(solution)/shard_map/reduce_scatter | solution.py:97
  1124.5 2.8 convert_element_type.246
  1127.3 33.9 %reduce-scatter.27.cloned.1.call-done = bf16[256,512]{0,1:T(8,128)(2,1)} async-done(((bf16[2048,512]{0,1:T(8,128)(2,1)}), bf16[256,512]{0,1:T(8,128)(2,1)}) %reduce-scatter.27.cloned.1.call-update) | async-done | bytes 262160 | tf_op jit(solution)/shard_map/reduce_scatter | solution.py:311
  1163.1 35.1 %reduce-scatter.29.cloned.1.call-done = bf16[512,256]{1,0:T(8,128)(2,1)} async-done(((bf16[512,2048]{1,0:T(8,128)(2,1)}), bf16[512,256]{1,0:T(8,128)(2,1)}) %reduce-scatter.29.cloned.1.call-update) | async-done | bytes 262160 | tf_op jit(solution)/shard_map/reduce_scatter | solution.py:314
  1199.9 35.1 %reduce-scatter.23.cloned.1.call-done = bf16[256,512]{0,1:T(8,128)(2,1)} async-done(((bf16[2048,512]{0,1:T(8,128)(2,1)}), bf16[256,512]{0,1:T(8,128)(2,1)}) %reduce-scatter.23.cloned.1.call-update) | async-done | bytes 262160 | tf_op jit(solution)/shard_map/reduce_scatter | solution.py:305
  1236.9 35.1 %reduce-scatter.25.cloned.1.call-done = bf16[256,512]{0,1:T(8,128)(2,1)} async-done(((bf16[2048,512]{0,1:T(8,128)(2,1)}), bf16[256,512]{0,1:T(8,128)(2,1)}) %reduce-scatter.25.cloned.1.call-update) | async-done | bytes 262160 | tf_op jit(solution)/shard_map/reduce_scatter | solution.py:308
  1273.9 52.2 %reduce-scatter.21.cloned.1.call-done = bf16[256,2048]{1,0:T(8,128)(2,1)} async-done(((bf16[1024,2048]{1,0:T(8,128)(2,1)}), bf16[256,2048]{1,0:T(8,128)(2,1)}) %reduce-scatter.21.cloned.1.call-update) | async-done | bytes 1048592 | tf_op jit(solution)/shard_map/reduce_scatter | solution.py:293
  1326.1 3.0 convert_add_fusion
  (227 shorter events, 54.2 us)
Async XLA Ops:
  7.2 3.5 copy-start.49
  7.2 17.0 %copy-start.43 = (s32[1024]{0:T(1024)S(1)}, s32[1024]{0:T(1024)}, u32[]{:S(2)}) copy-start(s32[1024]{0:T(1024)} %param.18) | copy-start | bytes 12292
  7.2 34.4 %all-gather.21.cloned.1.call-start = ((), (), s32[]{:S(2)}) async-start(), calls=%async_computation.16 | async-start | bytes 2359296 | tf_op jit(solution)/shard_map/all_gather | solution.py:122
  7.9 19.3 %copy-start.50 = (bf16[256]{0:T(256)(128)(2,1)S(1)}, bf16[256]{0:T(256)(128)(2,1)}, u32[]{:S(2)}) copy-start(bf16[256]{0:T(256)(128)(2,1)} %param.26) | copy-start | bytes 1540
  7.9 28.6 %copy-start.42 = (s32[1024]{0:T(1024)S(1)}, s32[1024]{0:T(1024)}, u32[]{:S(2)}) copy-start(s32[1024]{0:T(1024)} %param.17) | copy-start | bytes 12292
  8.0 87.5 %all-gather.15.cloned.1.call-start = ((), (), s32[]{:S(2)}) async-start(), calls=%async_computation.13 | async-start | bytes 5242880 | tf_op jit(solution)/shard_map/all_gather | solution.py:159
  8.7 117.5 %all-gather.19.cloned.1.call-start = ((), (), s32[]{:S(2)}) async-start(), calls=%async_computation.15 | async-start | bytes 2359296 | tf_op jit(solution)/shard_map/all_gather | solution.py:121
  9.4 147.3 %all-gather.17.cloned.1.call-start = ((), (), s32[]{:S(2)}) async-start(), calls=%async_computation.14 | async-start | bytes 2359296 | tf_op jit(solution)/shard_map/all_gather | solution.py:123
  10.0 177.7 %all-gather.23.cloned.1.call-start = ((), (), s32[]{:S(2)}) async-start(), calls=%async_computation.17 | async-start | bytes 2359296 | tf_op jit(solution)/shard_map/all_gather | solution.py:124
  10.6 234.9 %reduce-scatter.15.cloned.1.call-start = ((), (), s32[]{:S(2)}) async-start(), calls=%async_computation.18 | async-start | bytes 5242880 | tf_op jit(solution)/shard_map/reduce_scatter | solution.py:186
  36.4 106.3 %copy-start.35 = (f32[512]{0:T(512)}, f32[512]{0:T(512)S(1)}, u32[]{:S(2)}) copy-start(f32[512]{0:T(512)S(1)} %dynamic-slice_convert_fusion) | copy-start | bytes 6148
  36.5 107.1 %copy-start.37 = (f32[512]{0:T(512)}, f32[512]{0:T(512)S(1)}, u32[]{:S(2)}) copy-start(f32[512]{0:T(512)S(1)} %dynamic-slice_convert_fusion.1) | copy-start | bytes 6148
  100.7 42.1 %copy-start.5 = (f32[1024,512]{0,1:T(8,128)}, f32[1024,512]{0,1:T(8,128)S(1)}, u32[]{:S(2)}) copy-start(f32[1024,512]{0,1:T(8,128)S(1)} %get-tuple-element.152) | copy-start | bytes 6291460
  156.7 14.0 %copy-start.27 = (f32[4,1024]{1,0:T(4,128)}, f32[4,1024]{1,0:T(4,128)S(1)}, u32[]{:S(2)}) copy-start(f32[4,1024]{1,0:T(4,128)S(1)} %get-tuple-element.155) | copy-start | bytes 49156
  162.0 8.8 copy-start.19
  179.1 14.6 %copy-start.53 = (bf16[4,128,1024]{2,1,0:T(8,128)(2,1)}, bf16[4,128,1024]{2,1,0:T(8,128)(2,1)S(1)}, u32[]{:S(2)}) copy-start(bf16[4,128,1024]{2,1,0:T(8,128)(2,1)S(1)} %fusion.41) | copy-start | bytes 3145732
  193.7 2.3 copy-start.51
  193.7 53.3 %copy-start.13 = (bf16[256,2048]{1,0:T(8,128)(2,1)S(1)}, bf16[256,2048]{1,0:T(8,128)(2,1)}, u32[]{:S(2)}) copy-start(bf16[256,2048]{1,0:T(8,128)(2,1)} %param.15) | copy-start | bytes 3145732
  193.7 135.4 %all-gather.25.cloned.1.call-start = ((), (), s32[]{:S(2)}) async-start(), calls=%async_computation.19 | async-start | bytes 9437184 | tf_op jit(solution)/shard_map/all_gather | solution.py:125
  194.5 216.8 %all-gather.27.cloned.1.call-start = ((), (), s32[]{:S(2)}) async-start(), calls=%async_computation.20 | async-start | bytes 9437184 | tf_op jit(solution)/shard_map/all_gather | solution.py:126
  195.2 298.7 %all-gather.29.cloned.1.call-start = ((), (), s32[]{:S(2)}) async-start(), calls=%async_computation.21 | async-start | bytes 9437184 | tf_op jit(solution)/shard_map/all_gather | solution.py:127
  251.3 77.8 %all-to-all-start = ((bf16[4,256,2048]{2,1,0:T(8,128)(2,1)}), bf16[4,256,2048]{2,1,0:T(8,128)(2,1)}, u32[]{:S(2)}, u32[]{:S(2)}) async-start(bf16[4,256,2048]{2,1,0:T(8,128)(2,1)} %stack.27), calls=%async_computation.1 | async-start | bytes 8388608 | tf_op jit(solution)/shard_map/all_to_all | solution.py:196
  256.3 303.2 %reduce-scatter.17.cloned.1.call-start = ((), (), s32[]{:S(2)}) async-start(), calls=%async_computation.22 | async-start | bytes 5242880 | tf_op jit(solution)/shard_map/reduce_scatter | solution.py:204
  507.8 40.5 %copy-start.52 = (bf16[256]{0:T(256)(128)(2,1)S(1)}, bf16[256]{0:T(256)(128)(2,1)}, u32[]{:S(2)}) copy-start(bf16[256]{0:T(256)(128)(2,1)} %param.29) | copy-start | bytes 1540
  507.8 53.3 %copy-start.3 = (bf16[256,2048]{1,0:T(8,128)(2,1)S(1)}, bf16[256,2048]{1,0:T(8,128)(2,1)}, u32[]{:S(2)}) copy-start(bf16[256,2048]{1,0:T(8,128)(2,1)} %reduce-scatter.15.cloned.1.call-done) | copy-start | bytes 3145732
  507.8 113.3 %all-gather.31.cloned.1.call-start = ((), (), s32[]{:S(2)}) async-start(), calls=%async_computation.23 | async-start | bytes 5242880 | tf_op jit(solution)/shard_map/all_gather | solution.py:228
  561.1 5.8 copy-start.16
  566.9 155.4 %copy-start.1 = (f32[256,2048]{1,0:T(8,128)}, f32[256,2048]{1,0:T(8,128)S(1)}, u32[]{:S(2)}) copy-start(f32[256,2048]{1,0:T(8,128)S(1)} %get-tuple-element.121) | copy-start | bytes 6291460
  568.6 151.6 %reduce-scatter.19.cloned.1.call-start = ((), (), s32[]{:S(2)}) async-start(), calls=%async_computation.24 | async-start | bytes 5242880 | tf_op jit(solution)/shard_map/reduce_scatter | solution.py:236
  641.6 12.7 copy-start.55
  667.4 109.3 %all-gather.33.cloned.1.call-start = ((), (), s32[]{:S(2)}) async-start(), calls=%async_computation.25 | async-start | bytes 5242880 | tf_op jit(solution)/shard_map/all_gather | solution.py:251
  720.2 2.2 copy-start.14
  722.3 1.7 copy-start.28
  722.4 1.7 copy-start.34
  724.0 163.9 %reduce-scatter.37.cloned.1.call-start = ((), (), s32[]{:S(2)}) async-start(), calls=%async_computation.34 | async-start | bytes 589824
  782.0 14.6 %slice-start = ((s8[16777216]{0:T(1024)(128)(4,1)}), s8[4194304]{0:T(1024)(128)(4,1)S(1)}, s32[]{:S(2)}) async-start(s8[16777216]{0:T(1024)(128)(4,1)} %bitcast.111), calls=%async_computation.35 | async-start | bytes 8388608
  782.0 14.6 %slice-start.1 = ((s8[16777216]{0:T(1024)(128)(4,1)}), s8[4194304]{0:T(1024)(128)(4,1)S(1)}, s32[]{:S(2)}) async-start(s8[16777216]{0:T(1024)(128)(4,1)} %bitcast.111), calls=%async_computation.36 | async-start | bytes 8388608
  782.0 15.6 %slice-start.2 = ((s8[16777216]{0:T(1024)(128)(4,1)}), s8[4194304]{0:T(1024)(128)(4,1)S(1)}, s32[]{:S(2)}) async-start(s8[16777216]{0:T(1024)(128)(4,1)} %bitcast.111), calls=%async_computation.37 | async-start | bytes 8388608
  782.0 16.7 %slice-start.3 = ((s8[16777216]{0:T(1024)(128)(4,1)}), s8[4194304]{0:T(1024)(128)(4,1)S(1)}, s32[]{:S(2)}) async-start(s8[16777216]{0:T(1024)(128)(4,1)} %bitcast.111), calls=%async_computation.38 | async-start | bytes 8388608
  798.8 8.0 copy-start.12
  806.7 3.3 copy-start
  806.8 3.3 copy-start.10
  806.8 3.3 copy-start.21
  819.3 1.8 copy-start.6
  819.3 1.8 copy-start.30
  819.3 1.8 copy-start.36
  822.9 144.2 %reduce-scatter.31.cloned.1.call-start = ((), (), s32[]{:S(2)}) async-start(), calls=%async_computation.31 | async-start | bytes 9437184 | tf_op jit(solution)/shard_map/reduce_scatter | solution.py:91
  837.4 197.3 %reduce-scatter.33.cloned.1.call-start = ((), (), s32[]{:S(2)}) async-start(), calls=%async_computation.32 | async-start | bytes 9437184 | tf_op jit(solution)/shard_map/reduce_scatter | solution.py:94
  851.5 273.0 %reduce-scatter.35.cloned.1.call-start = ((), (), s32[]{:S(2)}) async-start(), calls=%async_computation.33 | async-start | bytes 9437184 | tf_op jit(solution)/shard_map/reduce_scatter | solution.py:97
  866.1 295.1 %reduce-scatter.27.cloned.1.call-start = ((), (), s32[]{:S(2)}) async-start(), calls=%async_computation.29 | async-start | bytes 2359296 | tf_op jit(solution)/shard_map/reduce_scatter | solution.py:311
  866.8 10.1 copy-start.44
  880.7 317.5 %reduce-scatter.29.cloned.1.call-start = ((), (), s32[]{:S(2)}) async-start(), calls=%async_computation.30 | async-start | bytes 2359296 | tf_op jit(solution)/shard_map/reduce_scatter | solution.py:314
  887.8 10.3 copy-start.39
  887.9 347.2 %reduce-scatter.23.cloned.1.call-start = ((), (), s32[]{:S(2)}) async-start(), calls=%async_computation.27 | async-start | bytes 2359296 | tf_op jit(solution)/shard_map/reduce_scatter | solution.py:305
  898.1 3.5 copy-start.45
  905.4 366.6 %reduce-scatter.25.cloned.1.call-start = ((), (), s32[]{:S(2)}) async-start(), calls=%async_computation.28 | async-start | bytes 2359296 | tf_op jit(solution)/shard_map/reduce_scatter | solution.py:308
  905.4 3.4 copy-start.46
  912.6 1.7 copy-start.48
  912.6 413.4 %reduce-scatter.21.cloned.1.call-start = ((), (), s32[]{:S(2)}) async-start(), calls=%async_computation.26 | async-start | bytes 5242880 | tf_op jit(solution)/shard_map/reduce_scatter | solution.py:293
  914.3 2.4 copy-start.25
  914.3 2.4 copy-start.47
  916.7 2.4 copy-start.18
  1124.5 201.6 %copy-start.15 = (bf16[256,2048]{1,0:T(8,128)(2,1)S(1)}, bf16[256,2048]{1,0:T(8,128)(2,1)}, u32[]{:S(2)}) copy-start(bf16[256,2048]{1,0:T(8,128)(2,1)} %reduce-scatter.19.cloned.1.call-done) | copy-start | bytes 3145732
  1127.3 198.8 %copy-start.2 = (f32[256,2048]{1,0:T(8,128)S(1)}, f32[256,2048]{1,0:T(8,128)}, u32[]{:S(2)}) copy-start(f32[256,2048]{1,0:T(8,128)} %copy-done.1) | copy-start | bytes 6291460
  (19 other events, 20.6 us)
Sparse Core Ops, SparseCore 0:
  9.6 31.9 all-gather.20
  43.4 51.9 all-gather.14
  97.0 29.1 all-gather.18
  127.7 28.5 all-gather.16
  157.7 29.9 all-gather.22
  193.8 51.6 reduce-scatter.14
  247.1 82.0 all-gather.24
  330.8 80.5 all-gather.26
  412.9 80.9 all-gather.28
  507.9 51.5 reduce-scatter.16
  568.7 52.3 all-gather.30
  667.5 52.5 reduce-scatter.18
  724.1 52.5 all-gather.32
  823.0 31.4 reduce-scatter.36
  856.7 87.6 reduce-scatter.30
  946.6 88.0 reduce-scatter.32
  1036.8 87.6 reduce-scatter.34
  1126.6 34.5 reduce-scatter.26
  1163.5 34.6 reduce-scatter.28
  1200.3 34.6 reduce-scatter.22
  1237.3 34.6 reduce-scatter.24
  1275.0 51.0 reduce-scatter.20
